TPU v7x, 128 devices: a whole 4x4x4 slice. The times are simulated.
128 devices in a mesh: req: 64 (over y, x, z), head: 2 (over core).
Axes of the slice: x: 4, y: 4, z: 4, core: 2. Of those that a mesh axis runs over, the one named last changes fastest.
Arguments:
- hidden_in: bfloat16 [4096, 2048], P('req'), may hold values from -14 to 14
- attn_gain: float32 [2048], replicated, may hold values from 0.1 to 1.9
- w_query: bfloat16 [2048, 2048], P(None, 'head'), may hold values from -0.125 to 0.125
- w_key: bfloat16 [2048, 1024], P(None, 'head'), may hold values from -0.125 to 0.125
- w_value: bfloat16 [2048, 1024], P(None, 'head'), may hold values from -0.125 to 0.125
- query_gain: float32 [128], replicated, may hold values from 0.5 to 2
- key_gain: float32 [128], replicated, may hold values from 0.5 to 2
- w_out: bfloat16 [2048, 2048], P('head'), may hold values from -0.125 to 0.125
- cache_keys: bfloat16 [64, 2048, 1024], P('req', None, 'head'), may hold values from -3.5 to 3.5
- cache_values: bfloat16 [64, 2048, 1024], P('req', None, 'head'), may hold values from -6 to 6
- cache_lengths: int32 [64], replicated, may hold values from 1 to 2048, 65536 in all
- slot_request: int32 [64], replicated, may hold values from 0 to 63, each once
- mlp_gain: float32 [2048], P('head'), may hold values from 0.1 to 1.9
- w_gate: bfloat16 [2048, 6144], P('head', 'req'), may hold values from -0.125 to 0.125
- w_up: bfloat16 [2048, 6144], P('head', 'req'), may hold values from -0.125 to 0.125
- w_down: bfloat16 [6144, 2048], P('req', 'head'), may hold values from -0.078125 to 0.078125
- final_gain: float32 [2048], replicated, may hold values from 0.1 to 1.9
- w_vocab: bfloat16 [2048, 151936], P(None, ('req', 'head')), may hold values from -8 to 8
Outputs:
- hidden_out: bfloat16 [4096, 2048], P('req', 'head')
- log_probs: float32 [64, 151936], P(None, ('req', 'head'))
Inputs may be any that keep to these rules, and one draw needn't show every extreme that they name: `cache_lengths`: the largest length is exactly 2048. `slot_request`: each request appears once.
All inputs are finite; a program needn't handle non-finite values.
Results may differ from a plain program's by a relative error of at most 0.008.
Values may be sent and summed in bfloat16 or wider, within the bound.
A program may use at most 128 MiB of HBM per device.

v0:
```python
import jax
import jax.numpy as jnp
from jax import lax
from jax.sharding import PartitionSpec as P

D = 2048
HEAD_DIM = 128
EPS = 1e-06
ROPE_BASE = 1000000.0
NEG = -1e30


def norm_rows(field, gain_vec):
    return field * lax.rsqrt(jnp.mean(field * field, axis=-1, keepdims=True) + EPS) * gain_vec


def rotate(field, positions):
    half_dim = field.shape[-1] // 2
    frequency = ROPE_BASE ** (-2.0 * jnp.arange(half_dim, dtype=jnp.float32) / field.shape[-1])
    angles = positions[..., None, None] * frequency
    cosine = jnp.cos(angles)
    sines = jnp.sin(angles)
    lower_half = field[..., :half_dim]
    upper_half = field[..., half_dim:]
    return jnp.concatenate(
        [lower_half * cosine - upper_half * sines, upper_half * cosine + lower_half * sines],
        axis=-1,
    )


def inverse_order(slot_request):
    indices = jnp.arange(slot_request.shape[0], dtype=jnp.int32)
    return jnp.sum(
        jnp.where(slot_request[None, :] == indices[:, None], indices[None, :], 0), axis=1
    )


def attend_slot(queries, keys_new, values_new, keys_cache, values_cache, cache_len):
    row_count, value_heads, head_size = keys_new.shape
    group_size = queries.shape[1] // value_heads
    grouped = queries.reshape(row_count, value_heads, group_size, head_size)
    score_scale = head_size ** (-0.5)
    recent = (
        jnp.einsum("skgd,tkd->kgst", grouped, keys_new, preferred_element_type=jnp.float32)
        * score_scale
    )
    causal = jnp.arange(row_count)[:, None] >= jnp.arange(row_count)[None, :]
    recent = jnp.where(causal, recent, NEG)
    cache_span = keys_cache.shape[0]
    stored = (
        jnp.einsum("skgd,lkd->kgsl", grouped, keys_cache, preferred_element_type=jnp.float32)
        * score_scale
    )
    stored = jnp.where(jnp.arange(cache_span, dtype=jnp.int32) < cache_len, stored, NEG)
    old_weights = jnp.exp(stored)
    new_weights = jnp.exp(recent)
    row_total = jnp.sum(old_weights, axis=-1) + jnp.sum(new_weights, axis=-1)
    old_weights = (old_weights / row_total[..., None]).astype(jnp.bfloat16)
    new_weights = (new_weights / row_total[..., None]).astype(jnp.bfloat16)
    blended = jnp.einsum(
        "kgsl,lkd->skgd", old_weights, values_cache, preferred_element_type=jnp.float32
    )
    blended = blended + jnp.einsum(
        "kgst,tkd->skgd", new_weights, values_new, preferred_element_type=jnp.float32
    )
    return blended.reshape(row_count, value_heads * group_size * head_size).astype(jnp.bfloat16)


def on_device(
    hidden_in,
    attn_gain,
    w_query,
    w_key,
    w_value,
    query_gain,
    key_gain,
    w_out,
    cache_keys,
    cache_values,
    cache_lengths,
    slot_request,
    mlp_gain,
    w_gate,
    w_up,
    w_down,
    final_gain,
    w_vocab,
):
    row_count = hidden_in.shape[0]
    half_width = mlp_gain.shape[0]
    slot_index = lax.axis_index("req")
    request_id = lax.dynamic_index_in_dim(slot_request, slot_index, 0, keepdims=False)
    cache_len = lax.dynamic_index_in_dim(cache_lengths, request_id, 0, keepdims=False)
    tokens = hidden_in.astype(jnp.float32)
    normed = norm_rows(tokens, attn_gain).astype(jnp.bfloat16)
    query_heads = w_query.shape[1] // HEAD_DIM
    value_heads = w_key.shape[1] // HEAD_DIM
    positions = (cache_len + jnp.arange(row_count, dtype=jnp.int32)).astype(jnp.float32)
    queries = jnp.dot(normed, w_query, preferred_element_type=jnp.float32).reshape(
        row_count, query_heads, HEAD_DIM
    )
    queries = rotate(norm_rows(queries, query_gain), positions).astype(jnp.bfloat16)
    keys_new = jnp.dot(normed, w_key, preferred_element_type=jnp.float32).reshape(
        row_count, value_heads, HEAD_DIM
    )
    keys_new = rotate(norm_rows(keys_new, key_gain), positions).astype(jnp.bfloat16)
    values_new = (
        jnp.dot(normed, w_value, preferred_element_type=jnp.float32)
        .astype(jnp.bfloat16)
        .reshape(row_count, value_heads, HEAD_DIM)
    )
    keys_cache = cache_keys.reshape(cache_keys.shape[1], value_heads, HEAD_DIM)
    values_cache = cache_values.reshape(cache_values.shape[1], value_heads, HEAD_DIM)
    attended = attend_slot(queries, keys_new, values_new, keys_cache, values_cache, cache_len)
    projected = jnp.dot(attended, w_out, preferred_element_type=jnp.float32)
    own_sum = lax.psum_scatter(
        projected.astype(jnp.bfloat16), "head", scatter_dimension=1, tiled=True
    ).astype(jnp.float32)
    head_part = lax.axis_index("head")
    residual = lax.dynamic_slice_in_dim(tokens, head_part * half_width, half_width, 1) + own_sum
    squares = lax.psum(jnp.sum(residual * residual, axis=1), "head")
    mixed_rows = (residual * lax.rsqrt(squares[:, None] / D + EPS) * mlp_gain).astype(jnp.bfloat16)
    paired = jnp.concatenate([w_gate, w_up], axis=1)
    partial_rows = jnp.dot(
        lax.all_gather(mixed_rows, "req", axis=0, tiled=True),
        paired,
        preferred_element_type=jnp.float32,
    )
    summed_rows = lax.psum(partial_rows.astype(jnp.bfloat16), "head").astype(jnp.float32)
    unit_count = w_gate.shape[1]
    active = (jax.nn.silu(summed_rows[:, :unit_count]) * summed_rows[:, unit_count:]).astype(
        jnp.bfloat16
    )
    down_part = lax.psum_scatter(
        jnp.dot(active, w_down, preferred_element_type=jnp.float32),
        "req",
        scatter_dimension=0,
        tiled=True,
    )
    output = residual + down_part
    hidden_out = output.astype(jnp.bfloat16)
    last_row = output[row_count - 1 :, :]
    collected = lax.all_gather(last_row, ("req", "head"), axis=1, tiled=True).reshape(-1, D)
    final_rows = norm_rows(collected, final_gain).astype(jnp.bfloat16)
    logits = jnp.dot(final_rows, w_vocab, preferred_element_type=jnp.float32)
    row_max = lax.pmax(jnp.max(logits, axis=1), ("req", "head"))
    row_total = lax.psum(jnp.sum(jnp.exp(logits - row_max[:, None]), axis=1), ("req", "head"))
    log_probs = logits - row_max[:, None] - jnp.log(row_total)[:, None]
    log_probs = jnp.take(log_probs, inverse_order(slot_request), axis=0)
    return (hidden_out, log_probs)


def solution(mesh):
    in_specs = (
        P("req", None),
        P(),
        P(None, "head"),
        P(None, "head"),
        P(None, "head"),
        P(),
        P(),
        P("head", None),
        P("req", None, "head"),
        P("req", None, "head"),
        P(),
        P(),
        P("head"),
        P("head", "req"),
        P("head", "req"),
        P("req", "head"),
        P(),
        P(None, ("req", "head")),
    )
    out_specs = (P("req", "head"), P(None, ("req", "head")))
    return jax.shard_map(
        on_device, mesh=mesh, in_specs=in_specs, out_specs=out_specs, check_vma=False
    )
```

profile of v0, /device:TPU:1, one launch (start us, length us, event | category | flops | bytes accessed | tf_op | source)
XLA Modules:
  0.0 747.4 jit_solution(8484590395757010456)
XLA Ops:
  7.2 1.4 dynamic_slice.11
  10.6 1.2 dynamic_slice.12
  11.8 0.6 add_convert_fusion.2
  12.5 0.7 iota_compare_fusion.2
  13.2 1.1 multiply_reduce_fusion.1
  14.3 3.2 convolution_bitcast_fusion
  18.5 4.0 reshape.165
  22.5 0.5 fusion.40
  23.5 4.1 reshape.167
  27.6 0.5 convolution_convert_fusion.2
  28.1 3.2 bitcast_reduce_fusion
  31.8 1.4 fusion.12
  33.7 3.8 convolution_convert_fusion.1
  37.6 14.1 %reduce-scatter.3.cloned.1.call-done = bf16[64,1024]{1,0:T(8,128)(2,1)} async-done(((bf16[64,2048]{1,0:T(8,128)(2,1)}), bf16[64,1024]{1,0:T(8,128)(2,1)}) %reduce-scatter.3.cloned.1.call-update) | async-done | bytes 131088 | tf_op jit(solution)/shard_map/reduce_scatter | solution.py:116
  51.6 1.0 multiply_reduce_fusion.2
  52.7 2.5 psum.21
  55.2 1.7 multiply_convert_fusion.3
  56.9 79.7 %all-gather.2.cloned.1.call-done = bf16[4096,1024]{1,0:T(8,128)(2,1)} async-done(((bf16[64,1024]{1,0:T(8,128)(2,1)}), bf16[4096,1024]{1,0:T(8,128)(2,1)}) %all-gather.2.cloned.1.call-update) | async-done | bytes 8388624 | tf_op jit(solution)/shard_map/all_gather | solution.py:125
  136.6 7.5 %convolution_convert_fusion = bf16[4096,192]{0,1:T(8,128)(2,1)} fusion(bf16[4096,1024]{1,0:T(8,128)(2,1)} %all-gather.2.cloned.1.call-done, bf16[1024,96]{0,1:T(8,128)(2,1)S(1)} %copy-done.12, bf16[1024,96]{0,1:T(8,128)(2,1)S(1)} %copy-done.13), kind=kOutput, calls=%fused_computation.1 | convolution fusion | flops 1612185600 | bytes 10354688 | tf_op jit(solution)/shard_map/dot_general | solution.py:124
  144.2 26.1 %all-reduce.2.cloned.1.call-done = bf16[4096,192]{0,1:T(8,128)(2,1)} async-done(((bf16[4096,192]{0,1:T(8,128)(2,1)}), bf16[4096,192]{0,1:T(8,128)(2,1)}) %all-reduce.2.cloned.1.call-update) | async-done | bytes 1572880 | tf_op jit(solution)/shard_map/psum | solution.py:129
  170.3 1.8 convert_element_type.67
  172.1 8.1 %fusion.18 = f32[4096,1024]{1,0:T(8,128)} fusion(bf16[96,1024]{1,0:T(8,128)(2,1)S(1)} %copy-done.6, f32[4096,192]{0,1:T(8,128)S(1)} %convert_element_type.67), kind=kOutput, calls=%fused_computation.24 | convolution fusion | flops 807665664 | bytes 20119552 | tf_op jit(solution)/shard_map/dot_general | solution.py:135
  180.2 0.6 copy-done.14
  181.0 339.7 %reduce-scatter.5.cloned.1.call-done = f32[64,1024]{1,0:T(8,128)} async-done(((f32[4096,1024]{1,0:T(8,128)}), f32[64,1024]{1,0:T(8,128)}) %reduce-scatter.5.cloned.1.call-update) | async-done | bytes 262160 | tf_op jit(solution)/shard_map/reduce_scatter | solution.py:134
  520.7 1.6 fusion.41
  522.4 81.9 %all_gather.7 = f32[1,131072]{1,0:T(1,128)S(1)} all-gather(f32[1,1024]{1,0:T(1,128)S(1)} %slice.36), channel_id=1, replica_groups=mesh['req'=64,'head'=2] {'req','head'}, dimensions={1}, use_global_device_ids=true | all-gather | bytes 528384 | tf_op jit(solution)/shard_map/all_gather | solution.py:143
  604.8 1.9 reduce.3
  606.9 4.2 fusion.44
  611.1 63.7 %pmax.7 = f32[64]{0:T(128)S(1)} all-reduce(f32[64]{0:T(128)S(1)} %get-tuple-element.14), channel_id=1, replica_groups=mesh['req'=64,'head'=2] {'req','head'}, use_global_device_ids=true, to_apply=%region_13.14 | all-reduce | flops 64 | bytes 512 | tf_op jit(solution)/shard_map/pmax | solution.py:146
  675.0 64.2 %psum.23 = f32[64]{0:T(128)S(1)} all-reduce(f32[64]{0:T(128)S(1)} %exponential_reduce_fusion), channel_id=1, replica_groups=mesh['req'=64,'head'=2] {'req','head'}, use_global_device_ids=true, to_apply=%region_15.16 | all-reduce | flops 64 | bytes 512 | tf_op jit(solution)/shard_map/psum | solution.py:147
  739.3 0.7 gather_fusion
  740.0 0.8 broadcast_select_fusion
  (76 shorter events, 3.8 us)
Async XLA Ops:
  7.2 15.3 %copy-start = (bf16[2048,512]{1,0:T(8,128)(2,1)S(1)}, bf16[2048,512]{1,0:T(8,128)(2,1)}, u32[]{:S(2)}) copy-start(bf16[2048,512]{1,0:T(8,128)(2,1)} %param.21) | copy-start | bytes 6291460
  7.2 10.9 %copy-start.10 = (f32[128]{0:T(128)S(1)}, f32[128]{0:T(128)}, u32[]{:S(2)}) copy-start(f32[128]{0:T(128)} %param.23) | copy-start | bytes 1540
  7.2 44.5 %reduce-scatter.3.cloned.1.call-start = ((), (), s32[]{:S(2)}) async-start(), calls=%async_computation.2 | async-start | bytes 393216 | tf_op jit(solution)/shard_map/reduce_scatter | solution.py:116
  17.7 4.8 copy-start.2
  17.7 4.8 copy-start.7
  18.4 4.8 copy-start.11
  23.0 4.6 copy-start.3
  28.1 3.6 copy-start.4
  33.6 21.6 %copy-start.9 = (f32[1024]{0:T(1024)S(1)}, f32[1024]{0:T(1024)}, u32[]{:S(2)}) copy-start(f32[1024]{0:T(1024)} %param.30) | copy-start | bytes 12292
  33.6 103.0 %copy-start.12 = (bf16[1024,96]{0,1:T(8,128)(2,1)S(1)}, bf16[1024,96]{0,1:T(8,128)(2,1)}, u32[]{:S(2)}) copy-start(bf16[1024,96]{0,1:T(8,128)(2,1)} %param.32) | copy-start | bytes 589828
  33.7 103.0 %copy-start.13 = (bf16[1024,96]{0,1:T(8,128)(2,1)S(1)}, bf16[1024,96]{0,1:T(8,128)(2,1)}, u32[]{:S(2)}) copy-start(bf16[1024,96]{0,1:T(8,128)(2,1)} %param.31) | copy-start | bytes 589828
  37.5 99.2 %all-gather.2.cloned.1.call-start = ((), (), s32[]{:S(2)}) async-start(), calls=%async_computation.3 | async-start | bytes 8519680 | tf_op jit(solution)/shard_map/all_gather | solution.py:125
  56.9 113.5 %all-reduce.2.cloned.1.call-start = ((), (), s32[]{:S(2)}) async-start(), calls=%async_computation.4 | async-start | bytes 3145728 | tf_op jit(solution)/shard_map/psum | solution.py:129
  144.2 27.9 %copy-start.6 = (bf16[96,1024]{1,0:T(8,128)(2,1)S(1)}, bf16[96,1024]{1,0:T(8,128)(2,1)}, u32[]{:S(2)}) copy-start(bf16[96,1024]{1,0:T(8,128)(2,1)} %param.33) | copy-start | bytes 589828
  144.2 376.5 %reduce-scatter.5.cloned.1.call-start = ((), (), s32[]{:S(2)}) async-start(), calls=%async_computation.5 | async-start | bytes 17039360 | tf_op jit(solution)/shard_map/reduce_scatter | solution.py:134
  180.2 0.7 copy-start.14
  180.2 340.5 %copy-start.5 = (bf16[64,1024]{1,0:T(8,128)(2,1)S(1)}, bf16[64,1024]{1,0:T(8,128)(2,1)}, u32[]{:S(2)}) copy-start(bf16[64,1024]{1,0:T(8,128)(2,1)} %reduce-scatter.3.cloned.1.call-done) | copy-start | bytes 393220
  180.9 426.0 %copy-start.8 = (f32[2048]{0:T(1024)S(1)}, f32[2048]{0:T(1024)}, u32[]{:S(2)}) copy-start(f32[2048]{0:T(1024)} %param.34) | copy-start | bytes 24580
  606.9 133.9 %copy-start.1 = (bf16[2048,512]{1,0:T(8,128)(2,1)S(1)}, bf16[2048,512]{1,0:T(8,128)(2,1)}, u32[]{:S(2)}) copy-start(bf16[2048,512]{1,0:T(8,128)(2,1)} %param.21) | copy-start | bytes 6291460
Sparse Core Ops, SparseCore 0:
  37.6 13.9 reduce-scatter.2
  57.0 79.6 all-gather.1
  144.3 25.9 all-reduce.1
  180.4 340.3 reduce-scatter.4
where the time goes:
time: 748 us; the launch traced here: 747 us
  waiting for transfers between devices  460 us (61%)
  blocking collectives  212 us (28%)
  matrix products  33.1 us (4%)
  between operations  16.1 us (2%)
  local copies, waits for them, and re-layouts  13.3 us (2%)
  other arithmetic  12.9 us (2%)
    reduce_scatter x1, waiting for transfers between devices, on_device(): lax.psum_scatter(jnp.dot(active, w_down, preferred_element_type=jnp.float...  340 us
    all_gather x1, blocking collectives, on_device(): lax.all_gather(last_row, ('req', 'head'), axis=1, tiled=True).reshape(-1, D)  81.9 us
    all_gather x1, waiting for transfers between devices, on_device(): lax.all_gather(mixed_rows, 'req', axis=0, tiled=True)  79.7 us
    psum x1, blocking collectives, on_device(): lax.psum(jnp.sum(jnp.exp(logits - row_max[:, None]), axis=1), ('req', 'he...  64.2 us
    pmax x1, blocking collectives, on_device(): row_max = lax.pmax(jnp.max(logits, axis=1), ('req', 'head'))  63.7 us
    psum x1, waiting for transfers between devices, on_device(): lax.psum(partial_rows.astype(jnp.bfloat16), 'head').astype(jnp.float32)  26.1 us
  transfers between devices with their start and end apart: 4, of which 4 were waited for; matrix products, arithmetic and copies ran while one was open for 0% of the time, Pallas kernels for 0%

commit v1 on v0

--- a/solution.py
+++ b/solution.py
@@ -122,7 +122,9 @@
     mixed_rows = (residual * lax.rsqrt(squares[:, None] / D + EPS) * mlp_gain).astype(jnp.bfloat16)
     paired = jnp.concatenate([w_gate, w_up], axis=1)
     partial_rows = jnp.dot(
-        lax.all_gather(mixed_rows, "req", axis=0, tiled=True),
+        jnp.concatenate(
+            lax.all_to_all(jnp.stack([mixed_rows] * lax.axis_size("req")), "req", 0, 0), axis=0
+        ),
         paired,
         preferred_element_type=jnp.float32,
     )

time: 748 us -> 772 us (1.032)
  blocking collectives: 212 us -> 317 us
  waiting for transfers between devices: 460 us -> 381 us
    all_to_all x0 -> x1, blocking collectives: none -> 106 us  [on_device(): lax.all_to_all(jnp.stack([mixed_rows] * lax.axis_size('req')), 'req', 0, 0)]
    all_gather x1 -> x0, waiting for transfers between devices: 79.7 us -> none  [on_device(): lax.all_gather(mixed_rows, 'req', axis=0, tiled=True)]
  transfers between devices with their start and end apart: 4 -> 3, of which waited for: 4 -> 3; matrix products, arithmetic and copies ran while one was open for 0% -> 0% of each run, Pallas kernels for 0% -> 0%
where the time goes in v1:
time: 772 us; the launch traced here: 771 us
  waiting for transfers between devices  381 us (49%)
  blocking collectives  317 us (41%)
  matrix products  29.6 us (4%)
  between operations  16.1 us (2%)
  local copies, waits for them, and re-layouts  14.3 us (2%)
  other arithmetic  12.2 us (2%)
    reduce_scatter x1, waiting for transfers between devices, on_device(): lax.psum_scatter(jnp.dot(active, w_down, preferred_element_type=jnp.float...  341 us
    all_to_all x1, blocking collectives, on_device(): lax.all_to_all(jnp.stack([mixed_rows] * lax.axis_size('req')), 'req', 0, 0)  106 us
    all_gather x1, blocking collectives, on_device(): lax.all_gather(last_row, ('req', 'head'), axis=1, tiled=True).reshape(-1, D)  80.9 us
    psum x1, blocking collectives, on_device(): lax.psum(jnp.sum(jnp.exp(logits - row_max[:, None]), axis=1), ('req', 'he...  64.2 us
    pmax x1, blocking collectives, on_device(): row_max = lax.pmax(jnp.max(logits, axis=1), ('req', 'head'))  63.6 us
    psum x1, waiting for transfers between devices, on_device(): lax.psum(partial_rows.astype(jnp.bfloat16), 'head').astype(jnp.float32)  26.6 us
  transfers between devices with their start and end apart: 3, of which 3 were waited for; matrix products, arithmetic and copies ran while one was open for 0% of the time, Pallas kernels for 0%

profile of v1, /device:TPU:1, one launch (start us, length us, event | category | flops | bytes accessed | tf_op | source)
XLA Modules:
  0.0 771.1 jit_solution(12899390756968501864)
XLA Ops:
  7.2 1.4 dynamic_slice.11
  10.6 1.2 dynamic_slice.12
  11.8 0.6 add_convert_fusion.2
  12.5 0.7 iota_compare_fusion.2
  13.2 1.1 multiply_reduce_fusion.1
  14.3 3.2 convolution_bitcast_fusion
  18.5 4.0 reshape.170
  23.5 4.1 reshape.172
  27.6 0.5 convolution_convert_fusion.2
  28.1 3.2 bitcast_reduce_fusion
  31.8 1.4 fusion.12
  33.6 3.7 convolution_convert_fusion.1
  37.5 14.1 %reduce-scatter.3.cloned.1.call-done = bf16[64,1024]{1,0:T(8,128)(2,1)} async-done(((bf16[64,2048]{1,0:T(8,128)(2,1)}), bf16[64,1024]{1,0:T(8,128)(2,1)}) %reduce-scatter.3.cloned.1.call-update) | async-done | bytes 131088 | tf_op jit(solution)/shard_map/reduce_scatter | solution.py:116
  51.6 1.0 multiply_reduce_fusion.2
  52.6 2.5 psum.21
  55.1 1.0 multiply_convert_fusion.3
  56.1 1.1 stack.2
  57.2 106.0 %all_to_all.5 = bf16[64,64,1024]{2,1,0:T(8,128)(2,1)S(1)} all-to-all(bf16[64,64,1024]{2,1,0:T(8,128)(2,1)S(1)} %stack.2), channel_id=1, replica_groups=mesh['req'=64,'head'=2] {'req'}, dimensions={0} | all-to-all | bytes 16777216 | tf_op jit(solution)/shard_map/all_to_all | solution.py:126
  163.2 4.0 convolution_convert_fusion
  167.5 26.6 %all-reduce.2.cloned.1.call-done = bf16[4096,192]{0,1:T(8,128)(2,1)} async-done(((bf16[4096,192]{0,1:T(8,128)(2,1)}), bf16[4096,192]{0,1:T(8,128)(2,1)}) %all-reduce.2.cloned.1.call-update) | async-done | bytes 1572880 | tf_op jit(solution)/shard_map/psum | solution.py:131
  194.1 1.8 convert_element_type.67
  195.9 8.1 %fusion.18 = f32[4096,1024]{1,0:T(8,128)} fusion(bf16[96,1024]{1,0:T(8,128)(2,1)S(1)} %copy-done.6, f32[4096,192]{0,1:T(8,128)S(1)} %convert_element_type.67), kind=kOutput, calls=%fused_computation.24 | convolution fusion | flops 807665664 | bytes 20119552 | tf_op jit(solution)/shard_map/dot_general | solution.py:137
  204.0 0.6 copy-done.14
  204.8 340.6 %reduce-scatter.5.cloned.1.call-done = f32[64,1024]{1,0:T(8,128)} async-done(((f32[4096,1024]{1,0:T(8,128)}), f32[64,1024]{1,0:T(8,128)}) %reduce-scatter.5.cloned.1.call-update) | async-done | bytes 262160 | tf_op jit(solution)/shard_map/reduce_scatter | solution.py:136
  545.4 1.6 fusion.41
  547.0 80.9 %all_gather.3 = f32[1,131072]{1,0:T(1,128)S(1)} all-gather(f32[1,1024]{1,0:T(1,128)S(1)} %slice.36), channel_id=1, replica_groups=mesh['req'=64,'head'=2] {'req','head'}, dimensions={1}, use_global_device_ids=true | all-gather | bytes 528384 | tf_op jit(solution)/shard_map/all_gather | solution.py:145
  628.5 1.9 reduce.3
  630.6 4.2 fusion.44
  634.8 63.6 %pmax.7 = f32[64]{0:T(128)S(1)} all-reduce(f32[64]{0:T(128)S(1)} %get-tuple-element.14), channel_id=1, replica_groups=mesh['req'=64,'head'=2] {'req','head'}, use_global_device_ids=true, to_apply=%region_13.14 | all-reduce | flops 64 | bytes 512 | tf_op jit(solution)/shard_map/pmax | solution.py:148
  698.7 64.2 %psum.23 = f32[64]{0:T(128)S(1)} all-reduce(f32[64]{0:T(128)S(1)} %exponential_reduce_fusion), channel_id=1, replica_groups=mesh['req'=64,'head'=2] {'req','head'}, use_global_device_ids=true, to_apply=%region_15.16 | all-reduce | flops 64 | bytes 512 | tf_op jit(solution)/shard_map/psum | solution.py:149
  763.0 0.7 gather_fusion
  763.7 0.8 broadcast_select_fusion
  (75 shorter events, 4.4 us)
Async XLA Ops:
  7.2 15.3 %copy-start = (bf16[2048,512]{1,0:T(8,128)(2,1)S(1)}, bf16[2048,512]{1,0:T(8,128)(2,1)}, u32[]{:S(2)}) copy-start(bf16[2048,512]{1,0:T(8,128)(2,1)} %param.21) | copy-start | bytes 6291460
  7.2 10.9 %copy-start.10 = (f32[128]{0:T(128)S(1)}, f32[128]{0:T(128)}, u32[]{:S(2)}) copy-start(f32[128]{0:T(128)} %param.23) | copy-start | bytes 1540
  7.2 44.4 %reduce-scatter.3.cloned.1.call-start = ((), (), s32[]{:S(2)}) async-start(), calls=%async_computation.3 | async-start | bytes 393216 | tf_op jit(solution)/shard_map/reduce_scatter | solution.py:116
  17.7 4.8 copy-start.2
  17.7 4.8 copy-start.7
  18.4 4.8 copy-start.11
  23.0 4.6 copy-start.3
  28.1 3.6 copy-start.4
  33.6 21.5 %copy-start.9 = (f32[1024]{0:T(1024)S(1)}, f32[1024]{0:T(1024)}, u32[]{:S(2)}) copy-start(f32[1024]{0:T(1024)} %param.30) | copy-start | bytes 12292
  37.4 156.7 %all-reduce.2.cloned.1.call-start = ((), (), s32[]{:S(2)}) async-start(), calls=%async_computation.4 | async-start | bytes 3145728 | tf_op jit(solution)/shard_map/psum | solution.py:131
  57.2 106.0 %copy-start.12 = (bf16[1024,96]{0,1:T(8,128)(2,1)S(1)}, bf16[1024,96]{0,1:T(8,128)(2,1)}, u32[]{:S(2)}) copy-start(bf16[1024,96]{0,1:T(8,128)(2,1)} %param.32) | copy-start | bytes 589828
  57.2 106.0 %copy-start.13 = (bf16[1024,96]{0,1:T(8,128)(2,1)S(1)}, bf16[1024,96]{0,1:T(8,128)(2,1)}, u32[]{:S(2)}) copy-start(bf16[1024,96]{0,1:T(8,128)(2,1)} %param.31) | copy-start | bytes 589828
  167.2 28.6 %copy-start.6 = (bf16[96,1024]{1,0:T(8,128)(2,1)S(1)}, bf16[96,1024]{1,0:T(8,128)(2,1)}, u32[]{:S(2)}) copy-start(bf16[96,1024]{1,0:T(8,128)(2,1)} %param.33) | copy-start | bytes 589828
  167.3 378.1 %reduce-scatter.5.cloned.1.call-start = ((), (), s32[]{:S(2)}) async-start(), calls=%async_computation.5 | async-start | bytes 17039360 | tf_op jit(solution)/shard_map/reduce_scatter | solution.py:136
  204.0 0.7 copy-start.14
  204.0 341.4 %copy-start.5 = (bf16[64,1024]{1,0:T(8,128)(2,1)S(1)}, bf16[64,1024]{1,0:T(8,128)(2,1)}, u32[]{:S(2)}) copy-start(bf16[64,1024]{1,0:T(8,128)(2,1)} %reduce-scatter.3.cloned.1.call-done) | copy-start | bytes 393220
  204.6 426.0 %copy-start.8 = (f32[2048]{0:T(1024)S(1)}, f32[2048]{0:T(1024)}, u32[]{:S(2)}) copy-start(f32[2048]{0:T(1024)} %param.34) | copy-start | bytes 24580
  630.6 133.9 %copy-start.1 = (bf16[2048,512]{1,0:T(8,128)(2,1)S(1)}, bf16[2048,512]{1,0:T(8,128)(2,1)}, u32[]{:S(2)}) copy-start(bf16[2048,512]{1,0:T(8,128)(2,1)} %param.21) | copy-start | bytes 6291460
Sparse Core Ops, SparseCore 0:
  37.5 13.9 reduce-scatter.2
  167.4 26.6 all-reduce.1
  204.1 341.2 reduce-scatter.4
